TPU v7x, 32 devices: a whole 2x2x4 slice. The times are simulated.
32 devices in a mesh: grp: 2 (over y), ctx: 4 (over x, core), head: 4 (over z).
Axes of the slice: x: 2, y: 2, z: 4, core: 2. Of those that a mesh axis runs over, the one named last changes fastest.
Arguments:
- prompt_hidden: bfloat16 [4, 1024, 4096], P('grp', 'ctx', 'head'), parts along dimension 0, may hold values from -3 to 3
- qkv_weight: bfloat16 [3, 4096, 4096], P(None, 'ctx', 'head'), may hold values from -0.09375 to 0.09375
- out_weight: bfloat16 [4096, 4096], P('head', 'ctx'), may hold values from -0.9375 to 0.9375
- embed_table: bfloat16 [32768, 4096], P('ctx', 'head'), may hold values from -60 to 60
- response_ids: int32 [4, 256], P(None, 'grp'), parts along dimension 1, may hold values from 0 to 32767
- assignment: int32 [256], P('grp'), parts along dimension 0, may hold values from 0 to 1
Outputs:
- final_hidden: bfloat16 [4, 256, 4096], P(None, ('grp', 'ctx'), 'head'), parts along dimension 1
There are 2 independent parts, one for each index of `grp`. A program takes and returns all parts, laid end to end along the dimension named above; an argument that names none is the same for every part. Nothing has to cross between parts.
All inputs are finite; a program needn't handle non-finite values.
Results may differ from a plain program's by a relative error of at most 0.023.
Values may be sent and summed in bfloat16 or wider, within the bound.
A program may use at most 128 MiB of HBM per device.

v0:
```python
import jax
import jax.numpy as jnp
from jax import lax
from jax.sharding import PartitionSpec as P

DH = 128


def rms_rows(values):
    return values * lax.rsqrt(jnp.mean(values * values, axis=-1, keepdims=True) + 1e-06)


def on_device(prompt_hidden, qkv_weight, out_weight, embed_table, response_ids, assignment):
    local_cols = prompt_hidden.shape[2]
    prompt_rows = prompt_hidden.shape[1]
    head_size = DH
    local_heads = local_cols // head_size
    steps = response_ids.shape[0]
    resp_local = response_ids.shape[1] // lax.axis_size("ctx")
    ctx_index = lax.axis_index("ctx")
    full_rows = lax.all_gather(qkv_weight, "ctx", axis=1, tiled=True)
    kv_weight = jnp.concatenate([full_rows[1], full_rows[2]], axis=1)
    piece = lax.all_gather(prompt_hidden, "head", axis=2, tiled=True)
    flat_piece = piece.reshape(2 * prompt_rows, piece.shape[2])
    kv_local = jnp.dot(flat_piece, kv_weight, preferred_element_type=jnp.float32)
    kv_local = kv_local.astype(jnp.bfloat16).reshape(2, prompt_rows, 2, local_heads, head_size)
    partial_state = jnp.einsum(
        "pthd,pthe->phde", kv_local[:, :, 0], kv_local[:, :, 1], preferred_element_type=jnp.float32
    )
    state = lax.psum(partial_state.astype(jnp.bfloat16), "ctx").astype(jnp.float32)
    vocab_rows = embed_table.shape[0]
    offset_ids = response_ids - ctx_index * vocab_rows
    inside = (offset_ids >= 0) & (offset_ids < vocab_rows)
    looked = jnp.take(embed_table, jnp.clip(offset_ids, 0, vocab_rows - 1), axis=0)
    looked = jnp.where(inside[:, :, None], looked.astype(jnp.float32), 0.0)
    embedded_mine = lax.psum_scatter(
        looked.astype(jnp.bfloat16), "ctx", scatter_dimension=1, tiled=True
    )
    embedded = lax.all_gather(embedded_mine, "head", axis=2, tiled=True)
    normed = rms_rows(embedded.astype(jnp.float32)).astype(jnp.bfloat16)
    projected_qkv = jnp.einsum(
        "trd,kde->trke", normed, full_rows, preferred_element_type=jnp.float32
    ).astype(jnp.bfloat16)
    projected_qkv = projected_qkv.reshape(steps, resp_local, 3, local_heads, head_size)
    query = projected_qkv[:, :, 0]
    key = projected_qkv[:, :, 1]
    value = projected_qkv[:, :, 2]
    my_prompt = lax.dynamic_slice_in_dim(assignment, ctx_index * resp_local, resp_local, 0)
    query_f = query.astype(jnp.float32)
    both = jnp.einsum("trhd,phde->ptrhe", query_f, state, precision=lax.Precision.HIGHEST)
    chosen = jnp.where((my_prompt == 0)[None, :, None, None], both[0], both[1])
    scores = jnp.einsum("trhd,srhd->rhts", query, key, preferred_element_type=jnp.float32)
    later = jnp.arange(steps)[:, None] >= jnp.arange(steps)[None, :]
    scores = jnp.where(later[None, None], scores, 0.0).astype(jnp.bfloat16)
    local = jnp.einsum("rhts,srhd->trhd", scores, value, preferred_element_type=jnp.float32)
    head_out = rms_rows(chosen + local).astype(jnp.bfloat16).reshape(steps, resp_local, local_cols)
    terms = jnp.einsum(
        "trd,de->tre",
        head_out,
        lax.all_gather(out_weight, "ctx", axis=1, tiled=True),
        preferred_element_type=jnp.float32,
    )
    width = terms.shape[2]
    mine = lax.psum_scatter(
        terms.astype(jnp.bfloat16), "head", scatter_dimension=2, tiled=True
    ).astype(jnp.float32)
    mixed = embedded_mine.astype(jnp.float32) + mine
    squares = lax.psum(jnp.sum(mixed * mixed, axis=-1), "head")
    result = mixed * lax.rsqrt(squares[:, :, None] / width + 1e-06)
    return result.astype(jnp.bfloat16)


def solution(mesh):
    return jax.shard_map(
        on_device,
        mesh=mesh,
        in_specs=(
            P("grp", "ctx", "head"),
            P(None, "ctx", "head"),
            P("head", "ctx"),
            P("ctx", "head"),
            P(None, "grp"),
            P("grp"),
        ),
        out_specs=P(None, ("grp", "ctx"), "head"),
        check_vma=False,
    )
```

profile of v0, /device:TPU:0, one launch (start us, length us, event | category | flops | bytes accessed | tf_op | source)
XLA Modules:
  0.0 461.3 jit_solution(4606842393122182999)
XLA Ops:
  6.5 0.7 compare_and_fusion.1
  7.9 10.7 %gather_fusion = bf16[512,1024]{1,0:T(8,128)(2,1)S(1)} fusion(bf16[8192,1024]{1,0:T(8,128)(2,1)} %param.9, s32[1024]{0:T(1024)S(1)} %pad_clamp_fusion), kind=kCustom, calls=%fused_computation | custom fusion | bytes 2099200 | tf_op jit(solution)/shard_map/jit(_take)/gather | solution.py:34
  18.6 1.4 select_convert_fusion
  20.0 0.7 all-gather.5.cloned.1.call-update
  21.5 26.1 %reduce-scatter.3.cloned.1.call-done = bf16[4,32,1024]{2,1,0:T(8,128)(2,1)} async-done(((bf16[4,128,1024]{2,1,0:T(8,128)(2,1)}), bf16[4,32,1024]{2,1,0:T(8,128)(2,1)}) %reduce-scatter.3.cloned.1.call-update) | async-done | bytes 262160 | tf_op jit(solution)/shard_map/reduce_scatter | solution.py:36
  47.9 156.1 %all-gather.5.cloned.1.call-done = bf16[3,4096,1024]{2,1,0:T(8,128)(2,1)} async-done(((bf16[3,1024,1024]{2,1,0:T(8,128)(2,1)}), bf16[3,4096,1024]{2,1,0:T(8,128)(2,1)}) %all-gather.5.cloned.1.call-update) | async-done | bytes 25165840 | tf_op jit(solution)/shard_map/all_gather | solution.py:21
  204.0 11.8 %slice_bitcast_fusion.1 = (bf16[4096,1024]{1,0:T(8,128)(2,1)}, bf16[4096,1024]{1,0:T(8,128)(2,1)}) fusion(bf16[3,4096,1024]{2,1,0:T(8,128)(2,1)} %all-gather.5.cloned.1.call-done), kind=kLoop, calls=%fused_computation.8 | loop fusion | bytes 33554432 | tf_op jit(solution)/shard_map/squeeze | solution.py:22
  215.9 70.5 %all-gather.7.cloned.1.call-done = bf16[2,256,4096]{2,1,0:T(8,128)(2,1)} async-done(((bf16[2,256,1024]{2,1,0:T(8,128)(2,1)}), bf16[2,256,4096]{2,1,0:T(8,128)(2,1)}) %all-gather.7.cloned.1.call-update) | async-done | bytes 4194320 | tf_op jit(solution)/shard_map/all_gather | solution.py:23
  286.4 17.3 %fusion.14 = bf16[512,2048]{0,1:T(8,128)(2,1)} fusion(bf16[512,4096]{1,0:T(8,128)(2,1)} %bitcast.86, bf16[4096,1024]{1,0:T(8,128)(2,1)} %get-tuple-element.8, bf16[4096,1024]{1,0:T(8,128)(2,1)} %get-tuple-element.7), kind=kOutput, calls=%fused_computation.13 | convolution fusion | flops 8624537600 | bytes 23068672 | tf_op jit(solution)/shard_map/dot_general | solution.py:25
  303.7 2.6 reshape.52
  306.3 1.5 slice_bitcast_fusion.3
  307.8 1.3 convolution_convert_fusion
  310.0 4.3 all-gather.9.cloned.1.call-done
  314.3 1.5 fusion.17
  315.9 12.1 %fusion.19 = bf16[4,32,3,1024]{3,1,2,0:T(8,128)(2,1)S(1)} fusion(bf16[3,4096,1024]{2,1,0:T(8,128)(2,1)} %all-gather.5.cloned.1.call-done, bf16[4,32,4096]{2,1,0:T(8,128)(2,1)} %all-gather.9.cloned.1.call-done, f32[4,32]{1,0:T(4,128)S(1)} %add_rsqrt_fusion.2), kind=kOutput, calls=%fused_computation.19 | convolution fusion | flops 3223191552 | bytes 27001344 | tf_op jit(solution)/shard_map/trd,kde->trke/dot_general | solution.py:41
  328.3 0.7 fusion.23
  329.0 20.3 %all-reduce.2.cloned.1.call-done = bf16[2,8,128,128]{3,2,0,1:T(8,128)(2,1)} async-done(((bf16[2,8,128,128]{3,2,0,1:T(8,128)(2,1)}), bf16[2,8,128,128]{3,2,0,1:T(8,128)(2,1)}) %all-reduce.2.cloned.1.call-update) | async-done | bytes 524304 | tf_op jit(solution)/shard_map/psum | solution.py:30
  349.3 1.3 convolution_bitcast_fusion
  351.1 58.0 %all-gather.11.cloned.1.call-done = bf16[1024,4096]{1,0:T(8,128)(2,1)} async-done(((bf16[1024,1024]{1,0:T(8,128)(2,1)}), bf16[1024,4096]{1,0:T(8,128)(2,1)}) %all-gather.11.cloned.1.call-update) | async-done | bytes 8388624 | tf_op jit(solution)/shard_map/all_gather | solution.py:60
  409.2 5.7 %fusion.8 = bf16[4,32,4096]{2,1,0:T(8,128)(2,1)} fusion(bf16[1024,4096]{1,0:T(8,128)(2,1)} %all-gather.11.cloned.1.call-done, f32[4,32,8,128]{3,1,0,2:T(8,128)S(1)} %get-tuple-element.6, f32[4,32,8]{1,0,2:T(4,128)S(1)} %add_rsqrt_fusion), kind=kOutput, calls=%fused_computation.11 | convolution fusion | flops 1074528256 | bytes 9965568 | tf_op jit(solution)/shard_map/trd,de->tre/dot_general | solution.py:57
  414.9 27.4 %reduce-scatter.5.cloned.1.call-done = bf16[4,32,1024]{2,1,0:T(8,128)(2,1)} async-done(((bf16[4,32,4096]{2,1,0:T(8,128)(2,1)}), bf16[4,32,1024]{2,1,0:T(8,128)(2,1)}) %reduce-scatter.5.cloned.1.call-update) | async-done | bytes 262160 | tf_op jit(solution)/shard_map/reduce_scatter | solution.py:64
  442.3 1.1 multiply_reduce_fusion
  443.4 9.3 %psum.15 = f32[4,32]{1,0:T(4,128)S(1)} all-reduce(f32[4,32]{1,0:T(4,128)S(1)} %multiply_reduce_fusion), channel_id=1, replica_groups=mesh['grp'=2,'ctx'=4,'head'=4] {'head'}, use_global_device_ids=true, to_apply=%region_6.7 | all-reduce | flops 128 | bytes 1024 | tf_op jit(solution)/shard_map/psum | solution.py:68
  452.7 1.8 multiply_convert_fusion
  (27 shorter events, 3.5 us)
Async XLA Ops:
  6.5 41.1 %reduce-scatter.3.cloned.1.call-start = ((), (), s32[]{:S(2)}) async-start(), calls=%async_computation.2 | async-start | bytes 1310720 | tf_op jit(solution)/shard_map/reduce_scatter | solution.py:36
  20.0 184.1 %all-gather.5.cloned.1.call-start = ((), (), s32[]{:S(2)}) async-start(), calls=%async_computation.3 | async-start | bytes 31457280 | tf_op jit(solution)/shard_map/all_gather | solution.py:21
  20.7 265.7 %all-gather.7.cloned.1.call-start = ((), (), s32[]{:S(2)}) async-start(), calls=%async_computation.4 | async-start | bytes 5242880 | tf_op jit(solution)/shard_map/all_gather | solution.py:23
  21.5 292.8 %all-gather.9.cloned.1.call-start = ((), (), s32[]{:S(2)}) async-start(), calls=%async_computation.6 | async-start | bytes 1310720 | tf_op jit(solution)/shard_map/all_gather | solution.py:39
  47.7 301.7 %all-reduce.2.cloned.1.call-start = ((), (), s32[]{:S(2)}) async-start(), calls=%async_computation.5 | async-start | bytes 1048576 | tf_op jit(solution)/shard_map/psum | solution.py:30
  303.7 6.2 %copy-start.1 = (s32[128]{0:T(128)S(1)}, s32[128]{0:T(128)}, u32[]{:S(2)}) copy-start(s32[128]{0:T(128)} %param.11) | copy-start | bytes 1540
  309.1 100.1 %all-gather.11.cloned.1.call-start = ((), (), s32[]{:S(2)}) async-start(), calls=%async_computation.7 | async-start | bytes 10485760 | tf_op jit(solution)/shard_map/all_gather | solution.py:60
  309.7 132.6 %reduce-scatter.5.cloned.1.call-start = ((), (), s32[]{:S(2)}) async-start(), calls=%async_computation.8 | async-start | bytes 1310720 | tf_op jit(solution)/shard_map/reduce_scatter | solution.py:64
  329.0 113.3 %copy-start = (bf16[4,32,1024]{2,1,0:T(8,128)(2,1)S(1)}, bf16[4,32,1024]{2,1,0:T(8,128)(2,1)}, u32[]{:S(2)}) copy-start(bf16[4,32,1024]{2,1,0:T(8,128)(2,1)} %reduce-scatter.3.cloned.1.call-done) | copy-start | bytes 786436
Sparse Core Ops, SparseCore 0:
  20.1 27.4 reduce-scatter.2
  49.2 154.7 all-gather.4
  205.6 80.7 all-gather.6
  287.8 26.4 all-gather.8
  316.5 32.7 all-reduce.1
  350.8 58.3 all-gather.10
  415.0 27.2 reduce-scatter.4
where the time goes:
time: 462 us; the launch traced here: 461 us
  waiting for transfers between devices  365 us (79%)
  matrix products  38.4 us (8%)
  local copies, waits for them, and re-layouts  26.9 us (6%)
  between operations  13.6 us (3%)
  blocking collectives  9.28 us (2%)
  other arithmetic  7.7 us (2%)
    all_gather x1, waiting for transfers between devices, on_device(): full_rows = lax.all_gather(qkv_weight, 'ctx', axis=1, tiled=True)  156 us
    all_gather x1, waiting for transfers between devices, on_device(): piece = lax.all_gather(prompt_hidden, 'head', axis=2, tiled=True)  70.5 us
    all_gather x1, waiting for transfers between devices, on_device(): lax.all_gather(out_weight, 'ctx', axis=1, tiled=True)  58 us
    reduce_scatter x1, waiting for transfers between devices, on_device(): lax.psum_scatter(terms.astype(jnp.bfloat16), 'head', scatter_dimension=2,...  27.4 us
    reduce_scatter x1, waiting for transfers between devices, on_device(): lax.psum_scatter(looked.astype(jnp.bfloat16), 'ctx', scatter_dimension=1,...  26.1 us
    psum x1, waiting for transfers between devices, on_device(): lax.psum(partial_state.astype(jnp.bfloat16), 'ctx').astype(jnp.float32)  20.3 us
    dot_general x1, matrix products, on_device(): jnp.dot(flat_piece, kv_weight, preferred_element_type=jnp.float32)  17.3 us
    dot_general x1, matrix products, on_device(): jnp.einsum('trd,kde->trke', normed, full_rows, preferred_element_type=jnp...  12.1 us
  transfers between devices with their start and end apart: 7, of which 7 were waited for; matrix products, arithmetic and copies ran while one was open for 11% of the time, Pallas kernels for 0%

commit v1 on v0

--- a/solution.py
+++ b/solution.py
@@ -20,7 +20,17 @@
     ctx_index = lax.axis_index("ctx")
     full_rows = lax.all_gather(qkv_weight, "ctx", axis=1, tiled=True)
     kv_weight = jnp.concatenate([full_rows[1], full_rows[2]], axis=1)
-    piece = lax.all_gather(prompt_hidden, "head", axis=2, tiled=True)
+    nodes = lax.axis_size("head")
+    local_part = sorted(((dev, (dev + 1) % nodes) for dev in range(nodes)))
+    tmp = prompt_hidden
+    rack = [tmp]
+    t = 1
+    while t < nodes:
+        tmp = lax.ppermute(tmp, "head", local_part)
+        rack.insert(0, tmp)
+        t = t + 1
+    now = jnp.concatenate(rack, 2)
+    piece = jnp.roll(now, (lax.axis_index("head") + 1) * prompt_hidden.shape[2], 2)
     flat_piece = piece.reshape(2 * prompt_rows, piece.shape[2])
     kv_local = jnp.dot(flat_piece, kv_weight, preferred_element_type=jnp.float32)
     kv_local = kv_local.astype(jnp.bfloat16).reshape(2, prompt_rows, 2, local_heads, head_size)

time: 462 us -> 381 us (0.82)
  waiting for transfers between devices: 365 us -> 280 us
    ppermute x0 -> x3, waiting for transfers between devices: none -> 76.4 us  [on_device(): tmp = lax.ppermute(tmp, 'head', local_part)]
    all_gather x1 -> x0, waiting for transfers between devices: 70.5 us -> none  [on_device(): piece = lax.all_gather(prompt_hidden, 'head', axis=2, tiled=True)]
    all_gather x1, waiting for transfers between devices: 156 us -> 98.2 us  [on_device(): full_rows = lax.all_gather(qkv_weight, 'ctx', axis=1, tiled=True)]
    reduce_scatter x1, waiting for transfers between devices: 26.1 us -> 0.01 us  [on_device(): lax.psum_scatter(looked.astype(jnp.bfloat16), 'ctx', scatter_dimension=1,...]
  transfers between devices with their start and end apart: 7 -> 9, of which waited for: 7 -> 7; matrix products, arithmetic and copies ran while one was open for 11% -> 14% of each run, Pallas kernels for 0% -> 0%
where the time goes in v1:
time: 381 us
  waiting for transfers between devices  280 us (73%)
  matrix products  37.2 us (10%)
  local copies, waits for them, and re-layouts  28.9 us (8%)
  between operations  13.7 us (4%)
  blocking collectives  9.28 us (2%)
  other arithmetic  7.72 us (2%)
    all_gather x1, waiting for transfers between devices, on_device(): full_rows = lax.all_gather(qkv_weight, 'ctx', axis=1, tiled=True)  98.2 us
    ppermute x3, waiting for transfers between devices, on_device(): tmp = lax.ppermute(tmp, 'head', local_part)  76.4 us
    all_gather x1, waiting for transfers between devices, on_device(): lax.all_gather(out_weight, 'ctx', axis=1, tiled=True)  58 us
    reduce_scatter x1, waiting for transfers between devices, on_device(): lax.psum_scatter(terms.astype(jnp.bfloat16), 'head', scatter_dimension=2,...  27.4 us
    psum x1, waiting for transfers between devices, on_device(): lax.psum(partial_state.astype(jnp.bfloat16), 'ctx').astype(jnp.float32)  18.9 us
    dot_general x1, matrix products, on_device(): jnp.dot(flat_piece, kv_weight, preferred_element_type=jnp.float32)  15.9 us
    dot_general x1, matrix products, on_device(): jnp.einsum('trd,kde->trke', normed, full_rows, preferred_element_type=jnp...  12.1 us
    squeeze x1, local copies, waits for them, and re-layouts, on_device(): kv_weight = jnp.concatenate([full_rows[1], full_rows[2]], axis=1)  11.6 us
  transfers between devices with their start and end apart: 9, of which 7 were waited for; matrix products, arithmetic and copies ran while one was open for 14% of the time, Pallas kernels for 0%

profile of v1, /device:TPU:0, one launch (start us, length us, event | category | flops | bytes accessed | tf_op | source)
XLA Modules:
  0.0 380.7 jit_solution(3156584296003578839)
XLA Ops:
  7.9 10.7 %gather_fusion = bf16[512,1024]{1,0:T(8,128)(2,1)S(1)} fusion(bf16[8192,1024]{1,0:T(8,128)(2,1)} %param.9, s32[1024]{0:T(1024)S(1)} %pad_clamp_fusion), kind=kCustom, calls=%fused_computation | custom fusion | bytes 2099200 | tf_op jit(solution)/shard_map/jit(_take)/gather | solution.py:44
  18.7 1.4 select_convert_fusion
  20.9 3.1 collective-permute-start
  24.0 25.2 %collective-permute-done = bf16[2,256,1024]{2,1,0:T(8,128)(2,1)S(1)} collective-permute-done((bf16[2,256,1024]{2,1,0:T(8,128)(2,1)S(1)}, bf16[2,256,1024]{2,1,0:T(8,128)(2,1)S(1)}, u32[]{:S(2)}, u32[]{:S(2)}) %collective-permute-start) | collective-permute-done | bytes 1048608 | tf_op jit(solution)/shard_map/ppermute | solution.py:29
  49.2 26.1 %collective-permute-done.1 = bf16[2,256,1024]{2,1,0:T(8,128)(2,1)S(1)} collective-permute-done((bf16[2,256,1024]{2,1,0:T(8,128)(2,1)S(1)}, bf16[2,256,1024]{2,1,0:T(8,128)(2,1)S(1)}, u32[]{:S(2)}, u32[]{:S(2)}) %collective-permute-start.1) | collective-permute-done | bytes 1048608 | tf_op jit(solution)/shard_map/ppermute | solution.py:29
  75.6 25.1 %collective-permute-done.2 = bf16[2,256,1024]{2,1,0:T(8,128)(2,1)} collective-permute-done((bf16[2,256,1024]{2,1,0:T(8,128)(2,1)S(1)}, bf16[2,256,1024]{2,1,0:T(8,128)(2,1)}, u32[]{:S(2)}, u32[]{:S(2)}) %collective-permute-start.2) | collective-permute-done | bytes 1048608 | tf_op jit(solution)/shard_map/ppermute | solution.py:29
  100.7 1.3 constant_dynamic-update-slice_fusion.7
  102.2 1.3 constant_dynamic-update-slice_fusion.3
  103.8 2.2 constant_dynamic-slice_fusion
  106.0 98.2 %all-gather.4.cloned.1.call-done = bf16[3,4096,1024]{2,1,0:T(8,128)(2,1)} async-done(((bf16[3,1024,1024]{2,1,0:T(8,128)(2,1)}), bf16[3,4096,1024]{2,1,0:T(8,128)(2,1)}) %all-gather.4.cloned.1.call-update) | async-done | bytes 25165840 | tf_op jit(solution)/shard_map/all_gather | solution.py:21
  204.2 11.6 %slice_bitcast_fusion.1 = (bf16[4096,1024]{1,0:T(8,128)(2,1)}, bf16[4096,1024]{1,0:T(8,128)(2,1)}) fusion(bf16[3,4096,1024]{2,1,0:T(8,128)(2,1)} %all-gather.4.cloned.1.call-done), kind=kLoop, calls=%fused_computation.8 | loop fusion | bytes 33554432 | tf_op jit(solution)/shard_map/squeeze | solution.py:22
  215.8 15.9 %fusion.16 = bf16[64,8,16,128]{3,1,2,0:T(8,128)(2,1)S(1)} fusion(bf16[512,4096]{1,0:T(8,128)(2,1)} %bitcast.86, bf16[4096,1024]{1,0:T(8,128)(2,1)} %get-tuple-element.8, bf16[4096,1024]{1,0:T(8,128)(2,1)} %get-tuple-element.7), kind=kOutput, calls=%fused_computation.18 | convolution fusion | flops 8624537600 | bytes 23068672 | tf_op jit(solution)/shard_map/dot_general | solution.py:35
  232.7 1.5 convolution_convert_fusion
  235.2 1.5 fusion.14
  236.7 12.1 %fusion.19 = bf16[4,32,3,1024]{3,1,2,0:T(8,128)(2,1)S(1)} fusion(bf16[3,4096,1024]{2,1,0:T(8,128)(2,1)} %all-gather.4.cloned.1.call-done, bf16[4,32,4096]{2,1,0:T(8,128)(2,1)} %all-gather.6.cloned.1.call-done, f32[4,32]{1,0:T(4,128)S(1)} %add_rsqrt_fusion.2), kind=kOutput, calls=%fused_computation.19 | convolution fusion | flops 3223191552 | bytes 27001344 | tf_op jit(solution)/shard_map/trd,kde->trke/dot_general | solution.py:51
  249.1 0.7 fusion.23
  249.9 18.9 %all-reduce.2.cloned.1.call-done = bf16[2,8,128,128]{3,2,0,1:T(8,128)(2,1)} async-done(((bf16[2,8,128,128]{3,2,0,1:T(8,128)(2,1)}), bf16[2,8,128,128]{3,2,0,1:T(8,128)(2,1)}) %all-reduce.2.cloned.1.call-update) | async-done | bytes 524304 | tf_op jit(solution)/shard_map/psum | solution.py:40
  268.8 1.3 convolution_bitcast_fusion
  270.6 58.0 %all-gather.8.cloned.1.call-done = bf16[1024,4096]{1,0:T(8,128)(2,1)} async-done(((bf16[1024,1024]{1,0:T(8,128)(2,1)}), bf16[1024,4096]{1,0:T(8,128)(2,1)}) %all-gather.8.cloned.1.call-update) | async-done | bytes 8388624 | tf_op jit(solution)/shard_map/all_gather | solution.py:70
  328.6 5.7 %fusion.8 = bf16[4,32,4096]{2,1,0:T(8,128)(2,1)} fusion(bf16[1024,4096]{1,0:T(8,128)(2,1)} %all-gather.8.cloned.1.call-done, f32[4,32,8,128]{3,1,0,2:T(8,128)S(1)} %get-tuple-element.6, f32[4,32,8]{1,0,2:T(4,128)S(1)} %add_rsqrt_fusion), kind=kOutput, calls=%fused_computation.11 | convolution fusion | flops 1074528256 | bytes 9965568 | tf_op jit(solution)/shard_map/trd,de->tre/dot_general | solution.py:67
  334.3 27.4 %reduce-scatter.5.cloned.1.call-done = bf16[4,32,1024]{2,1,0:T(8,128)(2,1)} async-done(((bf16[4,32,4096]{2,1,0:T(8,128)(2,1)}), bf16[4,32,1024]{2,1,0:T(8,128)(2,1)}) %reduce-scatter.5.cloned.1.call-update) | async-done | bytes 262160 | tf_op jit(solution)/shard_map/reduce_scatter | solution.py:74
  361.7 1.1 multiply_reduce_fusion
  362.8 9.3 %psum.15 = f32[4,32]{1,0:T(4,128)S(1)} all-reduce(f32[4,32]{1,0:T(4,128)S(1)} %multiply_reduce_fusion), channel_id=1, replica_groups=mesh['grp'=2,'ctx'=4,'head'=4] {'head'}, use_global_device_ids=true, to_apply=%region_6.7 | all-reduce | flops 128 | bytes 1024 | tf_op jit(solution)/shard_map/psum | solution.py:78
  372.1 1.8 multiply_convert_fusion
  (41 shorter events, 5.6 us)
Async XLA Ops:
  6.5 68.8 %reduce-scatter.3.cloned.1.call-start = ((), (), s32[]{:S(2)}) async-start(), calls=%async_computation.2 | async-start | bytes 1310720 | tf_op jit(solution)/shard_map/reduce_scatter | solution.py:46
  7.9 13.0 %copy-start = (bf16[2,256,1024]{2,1,0:T(8,128)(2,1)S(1)}, bf16[2,256,1024]{2,1,0:T(8,128)(2,1)}, u32[]{:S(2)}) copy-start(bf16[2,256,1024]{2,1,0:T(8,128)(2,1)} %param.6) | copy-start | bytes 3145732
  20.1 184.1 %all-gather.4.cloned.1.call-start = ((), (), s32[]{:S(2)}) async-start(), calls=%async_computation.3 | async-start | bytes 31457280 | tf_op jit(solution)/shard_map/all_gather | solution.py:21
  20.9 214.3 %all-gather.6.cloned.1.call-start = ((), (), s32[]{:S(2)}) async-start(), calls=%async_computation.5 | async-start | bytes 1310720 | tf_op jit(solution)/shard_map/all_gather | solution.py:49
  20.9 28.3 %collective-permute-start = (bf16[2,256,1024]{2,1,0:T(8,128)(2,1)S(1)}, bf16[2,256,1024]{2,1,0:T(8,128)(2,1)S(1)}, u32[]{:S(2)}, u32[]{:S(2)}) collective-permute-start(bf16[2,256,1024]{2,1,0:T(8,128)(2,1)S(1)} %copy-done), channel_id=1, source_target_pairs={{0,1},{1,2},{2,3},{3,0},{4,5},{5,6},{6,7},{7,4},{8,9},{9,10},{10,1... | collective-permute-start | bytes 3145736 | tf_op jit(solution)/shard_map/ppermute | solution.py:29
  49.2 26.1 %collective-permute-start.1 = (bf16[2,256,1024]{2,1,0:T(8,128)(2,1)S(1)}, bf16[2,256,1024]{2,1,0:T(8,128)(2,1)S(1)}, u32[]{:S(2)}, u32[]{:S(2)}) collective-permute-start(bf16[2,256,1024]{2,1,0:T(8,128)(2,1)S(1)} %collective-permute-done), channel_id=1, source_target_pairs={{0,1},{1,2},{2,3},{3,0},{4,5},{5,6},{6,7},{7,4},{8,9},{9,10},{10,1... | collective-permute-start | bytes 3145736 | tf_op jit(solution)/shard_map/ppermute | solution.py:29
  75.3 25.4 %collective-permute-start.2 = (bf16[2,256,1024]{2,1,0:T(8,128)(2,1)S(1)}, bf16[2,256,1024]{2,1,0:T(8,128)(2,1)}, u32[]{:S(2)}, u32[]{:S(2)}) collective-permute-start(bf16[2,256,1024]{2,1,0:T(8,128)(2,1)S(1)} %collective-permute-done.1), channel_id=1, source_target_pairs={{0,1},{1,2},{2,3},{3,0},{4,5},{5,6},{6,7},{7,4},{8,9},{9,10},{10,1... | collective-permute-start | bytes 3145736 | tf_op jit(solution)/shard_map/ppermute | solution.py:29
  75.4 193.4 %all-reduce.2.cloned.1.call-start = ((), (), s32[]{:S(2)}) async-start(), calls=%async_computation.4 | async-start | bytes 1048576 | tf_op jit(solution)/shard_map/psum | solution.py:40
  231.7 3.4 copy-start.2
  234.2 94.4 %all-gather.8.cloned.1.call-start = ((), (), s32[]{:S(2)}) async-start(), calls=%async_computation.6 | async-start | bytes 10485760 | tf_op jit(solution)/shard_map/all_gather | solution.py:70
  234.8 126.9 %reduce-scatter.5.cloned.1.call-start = ((), (), s32[]{:S(2)}) async-start(), calls=%async_computation.7 | async-start | bytes 1310720 | tf_op jit(solution)/shard_map/reduce_scatter | solution.py:74
  249.9 111.9 %copy-start.1 = (bf16[4,32,1024]{2,1,0:T(8,128)(2,1)S(1)}, bf16[4,32,1024]{2,1,0:T(8,128)(2,1)}, u32[]{:S(2)}) copy-start(bf16[4,32,1024]{2,1,0:T(8,128)(2,1)} %reduce-scatter.3.cloned.1.call-done) | copy-start | bytes 786436
Sparse Core Ops, SparseCore 0:
  20.2 27.4 reduce-scatter.2
  49.3 154.7 all-gather.3
  205.7 27.9 all-gather.5
  236.0 32.7 all-reduce.1
  270.2 58.3 all-gather.7
  334.4 27.2 reduce-scatter.4
